TPU v7x, 32 devices: a whole 2x2x4 slice. The times are simulated.
32 devices in a mesh: row: 8 (over y, x, core), col: 4 (over z).
Axes of the slice: x: 2, y: 2, z: 4, core: 2. Of those that a mesh axis runs over, the one named last changes fastest.
Arguments:
- pair_in: bfloat16 [384, 384, 128], P('row', 'col'), may hold values from -6 to 6
- coords: float32 [3, 384], P(None, 'row'), may hold values from -36 to 36
- chain_ids: int32 [384], P('row'), may hold values from 0 to 3, never falling along the last dimension, each value on 1 to 192 neighbouring positions
- coord_mask: int32 [384], P('row'), may hold values 0 or 1
- gain_tri: float32 [128], replicated, may hold values from 0.1 to 1.9
- gain_sum: float32 [128], replicated, may hold values from 0.1 to 1.9
- gain_attn: float32 [128], replicated, may hold values from 0.1 to 1.9
- w_tri_in: bfloat16 [128, 640], replicated, may hold values from -0.5 to 0.5
- w_tri_out: bfloat16 [128, 128], replicated, may hold values from -0.5 to 0.5
- w_bins: float32 [36, 128], replicated, may hold values from -3 to 3
- same_chain: float32 [128], replicated, may hold values from -6 to 6
- w_query: bfloat16 [128, 128], replicated, may hold values from -8 to 8
- w_attn: bfloat16 [128, 384], replicated, may hold values from -0.5 to 0.5
- w_bias: bfloat16 [128, 4], replicated, may hold values from -0.5 to 0.5
- w_attn_out: bfloat16 [128, 128], replicated, may hold values from -0.5 to 0.5
Outputs:
- pair_out: bfloat16 [384, 384, 128], P('row', 'col')
Inputs may be any that keep to these rules, and one draw needn't show every extreme that they name: `chain_ids`: chain numbers never fall along the residues, and no chain holds more than half of them.
All inputs are finite; a program needn't handle non-finite values. No bound on the sum of `coord_mask` on one device may be relied on, other than what follows from the above.
Results may differ from a plain program's by a relative error of at most 0.02.
Values may be sent and summed in bfloat16 or wider, within the bound.
A program may use at most 192 MiB of HBM per device.

v0:
```python
import math

import jax
import jax.numpy as jnp
from jax import lax
from jax.sharding import PartitionSpec as P


def layer_norm(values, gain):
    center = values - jnp.mean(values, axis=-1, keepdims=True)
    spread = jnp.mean(center * center, axis=-1, keepdims=True)
    return center * lax.rsqrt(spread + 1e-05) * gain


def body(
    pair_in,
    coords,
    chain_ids,
    coord_mask,
    gain_tri,
    gain_sum,
    gain_attn,
    w_tri_in,
    w_tri_out,
    w_bins,
    same_chain,
    w_query,
    w_attn,
    w_bias,
    w_attn_out,
):
    row_count, col_count, channels = pair_in.shape
    n_heads = w_bias.shape[1]
    head_size = channels // n_heads
    n_bins = w_bins.shape[0]
    col_start = lax.axis_index("col") * col_count
    coords_all, chains_all, masks_all = (
        lax.all_gather(coords, "row", axis=1, tiled=True),
        lax.all_gather(chain_ids, "row", axis=0, tiled=True),
        lax.all_gather(coord_mask, "row", axis=0, tiled=True),
    )
    pair_wide = pair_in.astype(jnp.float32)
    normed = layer_norm(pair_wide, gain_tri).astype(jnp.bfloat16)
    projected = jnp.dot(
        normed.reshape(row_count * col_count, channels),
        w_tri_in,
        preferred_element_type=jnp.float32,
    ).reshape(row_count, col_count, 5 * channels)
    left_side = (
        (jax.nn.sigmoid(projected[..., :channels]) * projected[..., channels : 2 * channels])
        .astype(jnp.bfloat16)
        .transpose(2, 0, 1)
    )
    right_side = (
        (
            jax.nn.sigmoid(projected[..., 2 * channels : 3 * channels])
            * projected[..., 3 * channels : 4 * channels]
        )
        .astype(jnp.bfloat16)
        .transpose(2, 0, 1)
    )
    tri_gate = jax.nn.sigmoid(projected[..., 4 * channels :])
    right_cols = lax.all_gather(right_side, "row", axis=1, tiled=True)
    summed = lax.psum_scatter(
        jnp.einsum("cjk,cik->jci", right_cols, left_side, preferred_element_type=jnp.float32),
        "col",
        scatter_dimension=0,
        tiled=True,
    )
    product = summed.transpose(2, 0, 1)
    summed_norm = layer_norm(product, gain_sum).astype(jnp.bfloat16)
    pair_one = pair_wide + tri_gate * jnp.dot(
        summed_norm.reshape(row_count * col_count, channels),
        w_tri_out,
        preferred_element_type=jnp.float32,
    ).reshape(row_count, col_count, channels)
    far_coords = lax.dynamic_slice_in_dim(coords_all, col_start, col_count, 1)
    far_chains = lax.dynamic_slice_in_dim(chains_all, col_start, col_count, 0)
    far_masks = lax.dynamic_slice_in_dim(masks_all, col_start, col_count, 0)
    offsets = coords[:, :, None] - far_coords[:, None, :]
    dist = jnp.sqrt(jnp.sum(offsets * offsets, axis=0) + 1.0)
    centres = 2.0 + 20.0 * jnp.arange(n_bins, dtype=jnp.float32) / (n_bins - 1)
    spacing = 25.0 / (n_bins - 1)
    pair_mask = coord_mask.astype(jnp.float32)[:, None] * far_masks.astype(jnp.float32)[None, :]
    feats = jnp.exp(-(((dist[..., None] - centres) / spacing) ** 2)) * pair_mask[..., None]
    binned = jnp.dot(
        feats.reshape(row_count * col_count, n_bins), w_bins, precision=lax.Precision.HIGHEST
    ).reshape(row_count, col_count, channels)
    shared = (chain_ids[:, None] == far_chains[None, :]).astype(jnp.float32)
    pair_two = (pair_one + binned + shared[..., None] * same_chain).astype(jnp.bfloat16)
    normed_two = layer_norm(pair_two.astype(jnp.float32), gain_attn).astype(jnp.bfloat16)
    flat_two = normed_two.reshape(row_count * col_count, channels)
    queries = (
        jnp.dot(flat_two, w_query, preferred_element_type=jnp.float32)
        .astype(jnp.bfloat16)
        .reshape(row_count, col_count, n_heads, head_size)
    )
    gate_pre = jnp.dot(
        flat_two, w_attn[:, 2 * channels :], preferred_element_type=jnp.float32
    ).reshape(row_count, col_count, channels)
    attn_gate = jax.nn.sigmoid(gate_pre)
    pair_bias = (
        jnp.dot(flat_two, w_bias, preferred_element_type=jnp.float32)
        .astype(jnp.bfloat16)
        .reshape(row_count, col_count, n_heads)
        .transpose(2, 0, 1)
    )
    bias_wide = lax.all_gather(pair_bias, "col", axis=2, tiled=True)
    bias_full = lax.all_gather(bias_wide, "row", axis=1, tiled=True)
    bias_mine = lax.dynamic_slice_in_dim(bias_full, col_start, col_count, 1)
    group = math.gcd(row_count, 8)
    blocks = row_count // group
    query_groups = queries.reshape(blocks, group, col_count, n_heads, head_size)
    root_dim = math.sqrt(head_size)
    start_state = (
        jnp.full((blocks, group, n_heads, col_count), -1e30, jnp.float32),
        jnp.zeros((blocks, group, n_heads, col_count), jnp.float32),
        jnp.zeros((blocks, group, n_heads, col_count, head_size), jnp.float32),
    )
    panel = lax.all_gather(normed_two, "col", axis=1, tiled=True)
    span = panel.shape[1]
    both = jnp.dot(
        panel.reshape(row_count * span, channels),
        w_attn[:, : 2 * channels],
        preferred_element_type=jnp.float32,
    ).reshape(row_count, span, 2 * channels)
    key_part = both[..., :channels].astype(jnp.bfloat16)
    span = key_part.shape[1]
    bias_part = bias_mine.astype(jnp.float32)
    key_groups = key_part.reshape(blocks, group, span, n_heads, head_size)
    value_groups = (
        both[..., channels:].astype(jnp.bfloat16).reshape(blocks, group, span, n_heads, head_size)
    )

    def one_block(items):
        query_blk, key_blk, value_blk, running_top, running_total, running_acc = items
        scores = (
            jnp.einsum("ijhd,ikhd->ihjk", query_blk, key_blk, preferred_element_type=jnp.float32)
            / root_dim
            + bias_part[None]
        )
        new_top = jnp.maximum(running_top, jnp.max(scores, axis=-1))
        rescale = jnp.exp(running_top - new_top)
        expo = jnp.exp(scores - new_top[..., None])
        new_total = running_total * rescale + jnp.sum(expo, axis=-1)
        new_acc = running_acc * rescale[..., None] + jnp.einsum(
            "ihjk,ikhd->ihjd",
            expo.astype(jnp.bfloat16),
            value_blk,
            preferred_element_type=jnp.float32,
        )
        return (new_top, new_total, new_acc)

    final_top, final_total, final_acc = lax.map(
        one_block,
        (query_groups, key_groups, value_groups, start_state[0], start_state[1], start_state[2]),
    )
    attended = (
        (final_acc / final_total[..., None])
        .reshape(row_count, n_heads, col_count, head_size)
        .transpose(0, 2, 1, 3)
        .reshape(row_count, col_count, channels)
    )
    gated = (attn_gate * attended).astype(jnp.bfloat16)
    result = pair_two.astype(jnp.float32) + jnp.dot(
        gated.reshape(row_count * col_count, channels),
        w_attn_out,
        preferred_element_type=jnp.float32,
    ).reshape(row_count, col_count, channels)
    return result.astype(jnp.bfloat16)


def solution(mesh):
    return jax.shard_map(
        body,
        mesh=mesh,
        in_specs=(
            P("row", "col", None),
            P(None, "row"),
            P("row"),
            P("row"),
            P(),
            P(),
            P(),
            P(),
            P(),
            P(),
            P(),
            P(),
            P(),
            P(),
            P(),
        ),
        out_specs=P("row", "col", None),
        check_vma=False,
    )
```

profile of v0, /device:TPU:0, one launch (start us, length us, event | category | flops | bytes accessed | tf_op | source)
XLA Modules:
  0.0 504.3 jit_solution(13640466424140914236)
XLA Ops:
  8.4 2.7 fusion.29
  13.2 2.7 fusion.57
  18.9 60.5 %all-gather.5.cloned.1.call-done = bf16[128,384,96]{0,2,1:T(8,128)(2,1)} async-done(((bf16[128,48,96]{0,2,1:T(8,128)(2,1)}), bf16[128,384,96]{0,2,1:T(8,128)(2,1)}) %all-gather.5.cloned.1.call-update) | async-done | bytes 9437200 | tf_op jit(solution)/shard_map/all_gather | solution.py:63
  79.4 15.5 %copy.76 = bf16[128,384,96]{2,1,0:T(8,128)(2,1)} copy(bf16[128,384,96]{0,2,1:T(8,128)(2,1)} %all-gather.5.cloned.1.call-done) | data formatting | bytes 18874368 | tf_op jit(solution)/shard_map/all_gather | solution.py:63
  95.0 13.6 %convolution_bitcast_fusion = f32[384,128,48]{0,2,1:T(8,128)} fusion(bf16[128,48,96]{2,1,0:T(8,128)(2,1)S(1)} %copy.75, bf16[128,384,96]{2,1,0:T(8,128)(2,1)} %copy.76), kind=kOutput, calls=%fused_computation.31 | convolution fusion | flops 452984832 | bytes 20054016 | tf_op jit(solution)/shard_map/cjk,cik->jci/dot_general | solution.py:65
  108.5 9.8 %copy.77 = f32[384,128,48]{1,2,0:T(8,128)} copy(f32[384,128,48]{0,2,1:T(8,128)} %convolution_bitcast_fusion) | data formatting | bytes 18874368 | tf_op jit(solution)/shard_map/cjk,cik->jci/transpose | solution.py:65
  119.0 8.9 %all-gather = f32[8,48,3]{1,2,0:T(4,128)S(1)} all-gather(f32[1,48,3]{1,2,0:T(4,128)S(1)} %bitcast.98), channel_id=1, replica_groups=mesh['row'=8,'col'=4] {'row'}, dimensions={0}, use_global_device_ids=true | all-gather | bytes 5184 | tf_op jit(solution)/shard_map/all_gather | solution.py:38
  129.7 7.0 %all-reduce.2 = (s32[384]{0:T(512)S(1)}, s32[384]{0:T(512)S(1)}) all-reduce(s32[384]{0:T(512)S(1)} %dynamic-update-slice.1, s32[384]{0:T(512)S(1)} %dynamic-update-slice), channel_id=1, replica_groups=mesh['row'=8,'col'=4] {'row'}, use_global_device_ids=true, to_apply=%add.1 | all-reduce | flops 768 | bytes 6144
  137.2 142.5 %reduce-scatter.2.cloned.1.call-done = f32[96,128,48]{1,2,0:T(8,128)} async-done(((f32[384,128,48]{1,2,0:T(8,128)}), f32[96,128,48]{1,2,0:T(8,128)}) %reduce-scatter.2.cloned.1.call-update) | async-done | bytes 2359312 | tf_op jit(solution)/shard_map/reduce_scatter | solution.py:64
  279.7 2.5 bitcast_reduce_fusion
  286.8 7.1 %convert_reduce_fusion = (f32[48,96]{1,0:T(8,128)S(1)}, bf16[48,96,128]{2,1,0:T(8,128)(2,1)S(1)}) fusion(f32[128]{0:T(128)S(1)} %copy-done.20, f32[48,96]{1,0:T(8,128)S(1)} %compare_convert_fusion, f32[36,128]{1,0:T(8,128)S(1)} %copy-done.18, f32[48,96]{1,0:T(8,128)S(1)} %get-tuple-element.114, f32[36]{0:T(128)S(1)} %multiply_add_fusion.1, ...), kind=kOutput, calls=%fused_computation.27 | convolution fusion | flops 262706688 | bytes 7170704 | tf_op jit(solution)/shard_map/dot_general | solution.py:86
  297.8 15.3 %all_gather.26 = bf16[4,48,384]{1,0,2:T(4,128)(2,1)S(1)} all-gather(bf16[4,48,96]{1,0,2:T(4,128)(2,1)S(1)} %bitcast.97), channel_id=1, replica_groups=mesh['row'=8,'col'=4] {'col'}, dimensions={2}, use_global_device_ids=true | all-gather | bytes 184320 | tf_op jit(solution)/shard_map/all_gather | solution.py:108
  318.5 20.2 %all-gather.9.cloned.1.call-done = bf16[4,384,384]{2,0,1:T(4,128)(2,1)} async-done(((bf16[4,48,384]{2,0,1:T(4,128)(2,1)}), bf16[4,384,384]{2,0,1:T(4,128)(2,1)}) %all-gather.9.cloned.1.call-update) | async-done | bytes 1179664 | tf_op jit(solution)/shard_map/all_gather | solution.py:109
  339.8 89.8 %all-gather.7.cloned.1.call-done = bf16[48,384,128]{2,1,0:T(8,128)(2,1)} async-done(((bf16[48,96,128]{2,1,0:T(8,128)(2,1)}), bf16[48,384,128]{2,1,0:T(8,128)(2,1)}) %all-gather.7.cloned.1.call-update) | async-done | bytes 4718608 | tf_op jit(solution)/shard_map/all_gather | solution.py:120
  429.6 8.6 %convolution_convert_fusion = bf16[48,384,256]{1,2,0:T(8,128)(2,1)} fusion(bf16[48,384,128]{2,1,0:T(8,128)(2,1)} %all-gather.7.cloned.1.call-done, bf16[128,384]{1,0:T(8,128)(2,1)} %param.29), kind=kOutput, calls=%fused_computation.22 | convolution fusion | flops 1212678144 | bytes 14221312 | tf_op jit(solution)/shard_map/dot_general | solution.py:122
  438.2 9.3 %fusion.82 = (bf16[48,384,128]{1,2,0:T(8,128)(2,1)}, bf16[48,384,128]{1,2,0:T(8,128)(2,1)}) fusion(bf16[48,384,256]{1,2,0:T(8,128)(2,1)} %convolution_convert_fusion), kind=kLoop, calls=%fused_computation.112 | loop fusion | bytes 18874368 | tf_op jit(solution)/shard_map/slice | solution.py:132
  447.4 41.3 %while.12 = (s32[]{:T(128)}, f32[6,8,4,96]{3,2,1,0:T(4,128)S(1)}, f32[6,8,4,96,32]{3,4,2,1,0:T(8,128)}, bf16[6,8,96,4,32]{2,1,0,4,3:T(8,128)(2,1)S(1)}, bf16[6,8...) while((s32[]{:T(128)}, f32[6,8,4,96]{3,2,1,0:T(4,128)S(1)}, ...), condition=%wide.region_11.12_spmd, body=%wide.region_8.11_spmd.sunk | while | flops 164084736 | bytes 18761308 | solution.py:154
  447.5 2.1 fusion.97
  449.6 3.1 fusion.99
  454.4 2.1 fusion.97
  456.4 3.1 fusion.99
  461.2 2.1 fusion.97
  463.3 3.1 fusion.99
  468.1 2.1 fusion.97
  470.2 3.1 fusion.99
  475.0 2.1 fusion.97
  477.1 3.1 fusion.99
  481.9 2.1 fusion.97
  484.0 3.1 fusion.99
  488.7 2.4 broadcast_divide_fusion
  491.1 2.2 copy.90
  493.3 4.4 fusion.35
  (120 shorter events, 33.9 us)
Async XLA Ops:
  6.5 4.6 copy-start
  6.5 4.6 copy-start.5
  6.5 4.6 copy-start.12
  6.5 72.9 %all-gather.5.cloned.1.call-start = ((), (), s32[]{:S(2)}) async-start(), calls=%async_computation.1 | async-start | bytes 10616832 | tf_op jit(solution)/shard_map/all_gather | solution.py:63
  13.2 4.6 copy-start.2
  17.9 261.8 %reduce-scatter.2.cloned.1.call-start = ((), (), s32[]{:S(2)}) async-start(), calls=%async_computation.2 | async-start | bytes 11796480 | tf_op jit(solution)/shard_map/reduce_scatter | solution.py:64
  118.3 0.7 copy-start.10
  118.3 9.6 %copy-start.19 = (s32[48]{0:T(128)S(1)}, s32[48]{0:T(128)}, u32[]{:S(2)}) copy-start(s32[48]{0:T(128)} %param.20) | copy-start | bytes 580
  118.3 9.6 %copy-start.21 = (u32[32]{0:T(128)S(1)}, u32[32]{0:T(128)}, u32[]{:S(2)}) copy-start(u32[32]{0:T(128)} %constant.69) | copy-start | bytes 388
  118.3 11.1 %copy-start.13 = (s32[48]{0:T(128)S(1)}, s32[48]{0:T(128)}, u32[]{:S(2)}) copy-start(s32[48]{0:T(128)} %param.19) | copy-start | bytes 580
  118.4 220.4 %all-gather.9.cloned.1.call-start = ((), (), s32[]{:S(2)}) async-start(), calls=%async_computation.4 | async-start | bytes 1327104 | tf_op jit(solution)/shard_map/all_gather | solution.py:109
  137.2 146.8 %copy-start.16 = (f32[128]{0:T(128)S(1)}, f32[128]{0:T(128)}, u32[]{:S(2)}) copy-start(f32[128]{0:T(128)} %param.22) | copy-start | bytes 1540
  279.7 2.7 copy-start.3
  283.8 1.7 copy-start.8
  285.5 1.3 copy-start.6
  285.5 1.3 copy-start.18
  285.5 1.3 copy-start.20
  286.8 8.8 %copy-start.14 = (f32[128]{0:T(128)S(1)}, f32[128]{0:T(128)}, u32[]{:S(2)}) copy-start(f32[128]{0:T(128)} %param.23) | copy-start | bytes 1540
  293.9 1.7 copy-start.7
  293.9 3.2 copy-start.11
  297.1 17.2 %copy-start.4 = (bf16[48,96,128]{2,1,0:T(8,128)(2,1)}, bf16[48,96,128]{2,1,0:T(8,128)(2,1)S(1)}, u32[]{:S(2)}) copy-start(bf16[48,96,128]{2,1,0:T(8,128)(2,1)S(1)} %fusion.28) | copy-start | bytes 3538948
  297.1 17.5 %copy-start.9 = (bf16[128,128]{1,0:T(8,128)(2,1)S(1)}, bf16[128,128]{1,0:T(8,128)(2,1)}, u32[]{:S(2)}) copy-start(bf16[128,128]{1,0:T(8,128)(2,1)} %param.28) | copy-start | bytes 98308
  314.0 115.6 %all-gather.7.cloned.1.call-start = ((), (), s32[]{:S(2)}) async-start(), calls=%async_computation.3 | async-start | bytes 5898240 | tf_op jit(solution)/shard_map/all_gather | solution.py:120
  491.1 2.2 copy-start.15
  491.1 2.2 copy-start.17
  493.3 4.4 copy-start.1
Sparse Core Ops, SparseCore 0:
  18.0 61.4 all-gather.4
  118.5 161.1 reduce-scatter.1
  314.1 24.5 all-gather.8
  340.1 89.3 all-gather.6
where the time goes:
time: 506 us; the launch traced here: 504 us
  waiting for transfers between devices  313 us (62%)
  matrix products  69.3 us (14%)
  local copies, waits for them, and re-layouts  46.4 us (9%)
  blocking collectives  31.1 us (6%)
  other arithmetic  29.3 us (6%)
  between operations  14.2 us (3%)
    reduce_scatter x1, waiting for transfers between devices, body(): lax.psum_scatter(jnp.einsum('cjk,cik->jci', right_cols, left_side, prefer...  142 us
    all_gather x1, waiting for transfers between devices, body(): panel = lax.all_gather(normed_two, 'col', axis=1, tiled=True)  89.8 us
    all_gather x1, waiting for transfers between devices, body(): right_cols = lax.all_gather(right_side, 'row', axis=1, tiled=True)  60.5 us
    all_gather x1, waiting for transfers between devices, body(): bias_full = lax.all_gather(bias_wide, 'row', axis=1, tiled=True)  20.2 us
    dot_general x6, matrix products, one_block(): jnp.einsum('ihjk,ikhd->ihjd', expo.astype(jnp.bfloat16), value_blk, prefe...  18.7 us
    all_gather x1, local copies, waits for them, and re-layouts, body(): right_cols = lax.all_gather(right_side, 'row', axis=1, tiled=True)  15.5 us
    all_gather x1, blocking collectives, body(): bias_wide = lax.all_gather(pair_bias, 'col', axis=2, tiled=True)  15.3 us
    dot_general x1, matrix products, body(): jnp.einsum('cjk,cik->jci', right_cols, left_side, preferred_element_type=...  13.6 us
  transfers between devices with their start and end apart: 4, of which 4 were waited for; matrix products, arithmetic and copies ran while one was open for 2% of the time, Pallas kernels for 0%

commit v1 on v0

v1 whole, which is shorter than its diff:
```python
import functools
import math

import jax
import jax.numpy as jnp
from jax import lax
from jax.experimental import pallas as pl
from jax.experimental.pallas import tpu as pltpu
from jax.sharding import PartitionSpec as P

MESH = pl.DeviceIdType.MESH
LOG2E = math.log2(math.e)
PIECES = 2


def contract_last(a, b):
    return lax.dot_general(a, b, (((1,), (1,)), ((), ())), preferred_element_type=jnp.float32)


def attend_kernel(
    n_row,
    n_col,
    n_heads,
    normed_ref,
    bias_ref,
    pair_ref,
    wq_ref,
    wk_ref,
    wvt_ref,
    wg_ref,
    wo_ref,
    out_ref,
    blocks,
    land,
    bias_all,
    bias_full,
    q_wide,
    top,
    total,
    acc,
    hop1_send,
    hop1_recv,
    hop2_send,
    hop2_recv,
    hop3_send,
    hop3_recv,
    copy_sem,
    right_send,
    left_send,
    block_recv,
):
    row = lax.axis_index("row")
    col = lax.axis_index("col")
    rows, cols, channels = normed_ref.shape
    halves = cols // rows
    head = channels // n_heads
    wide = cols * n_heads
    strip = rows * n_heads
    core = lax.rem(row, halves)
    home = row // halves
    groups = n_row // halves
    part = rows // PIECES

    barrier = pltpu.get_barrier_semaphore()
    for step in range(1, n_row):
        pl.semaphore_signal(
            barrier, inc=1, device_id=(lax.rem(row + step, n_row), col), device_id_type=MESH
        )
    for step in range(1, n_col):
        pl.semaphore_signal(
            barrier, inc=1, device_id=(row, lax.rem(col + step, n_col)), device_id_type=MESH
        )
    pl.semaphore_wait(barrier, n_row - 1 + n_col - 1)

    def hop1(source):
        return pltpu.make_async_remote_copy(
            src_ref=bias_ref,
            dst_ref=land.at[source],
            send_sem=hop1_send,
            recv_sem=hop1_recv.at[source],
            device_id=(row, home),
            device_id_type=MESH,
        )

    @pl.when(col != home)
    def _():
        hop1(col).start()

    def piece_copy(owner, piece, own, to_right):
        at = pl.ds(piece * part, part)
        source = normed_ref.at[at] if own else blocks.at[owner, at]
        sems = right_send if to_right else left_send
        return pltpu.make_async_remote_copy(
            src_ref=source,
            dst_ref=blocks.at[owner, at],
            send_sem=sems.at[owner, piece],
            recv_sem=block_recv.at[owner, piece],
            device_id=(row, col + 1 if to_right else col - 1),
            device_id_type=MESH,
        )

    for piece in range(PIECES):

        @pl.when(col < n_col - 1)
        def _():
            piece_copy(col, piece, True, True).start()

        @pl.when(col > 0)
        def _():
            piece_copy(col, piece, True, False).start()

    lane = lax.broadcasted_iota(jnp.int32, (rows, channels), 1) // head

    def make_queries(i, carry):
        query = jnp.dot(normed_ref[i], wq_ref[...], preferred_element_type=jnp.float32)
        for half in range(halves):
            mine = query[half * rows : (half + 1) * rows]
            for h in range(n_heads):
                start = half * strip + h * rows
                q_wide[i, start : start + rows, :] = jnp.where(lane == h, mine, 0.0).astype(
                    jnp.bfloat16
                )
        return carry

    lax.fori_loop(0, rows, make_queries, 0, unroll=2)

    def hop2(step):
        return pltpu.make_async_remote_copy(
            src_ref=land,
            dst_ref=bias_all.at[core],
            send_sem=hop2_send.at[step],
            recv_sem=hop2_recv,
            device_id=(lax.rem(home + step, groups) * halves + core, col),
            device_id_type=MESH,
        )

    def hop3(slot):
        return pltpu.make_async_remote_copy(
            src_ref=bias_all.at[slot],
            dst_ref=bias_all.at[slot],
            send_sem=hop3_send,
            recv_sem=hop3_recv,
            device_id=(home * halves + (1 - core), col),
            device_id_type=MESH,
        )

    @pl.when(col == home)
    def _():
        own = pltpu.make_async_copy(bias_ref, land.at[col], copy_sem)
        own.start()
        own.wait()
        for step in range(1, n_col):
            hop1(lax.rem(col + step, n_col)).wait_recv()
        for step in range(1, groups):
            hop2(step).start()
        keep = pltpu.make_async_copy(land, bias_all.at[core], copy_sem)
        keep.start()
        keep.wait()

    @pl.when(col != home)
    def _():
        hop2(1).wait_recv()

    hop3(core).start()
    hop3(1 - core).wait_recv()

    for k in range(n_col):
        for half in range(halves):
            bias_full[k, :, half * strip : (half + 1) * strip] = (
                bias_all[half, k].astype(jnp.float32) * LOG2E
            )

    lane_head = lax.rem(lax.broadcasted_iota(jnp.int32, (head, wide), 1), strip) // rows
    factor = LOG2E / math.sqrt(head)

    def attend(block, owner, i, first):
        keys = jnp.dot(block, wk_ref[...], preferred_element_type=jnp.float32).astype(jnp.bfloat16)
        values = contract_last(wvt_ref[...], block).astype(jnp.bfloat16)
        scores = contract_last(keys, q_wide[i]) * factor + bias_full[owner]
        peak = jnp.max(scores, axis=0, keepdims=True)
        if not first:
            old = top[i]
            peak = jnp.maximum(old, peak)
            shrink = jnp.exp2(old - peak)
        expo = jnp.exp2(scores - peak)
        summed = jnp.sum(expo, axis=0, keepdims=True)
        mixed = jnp.dot(values, expo.astype(jnp.bfloat16), preferred_element_type=jnp.float32)
        picked = mixed[:head]
        for h in range(1, n_heads):
            picked = jnp.where(lane_head == h, mixed[h * head : (h + 1) * head], picked)
        top[i] = peak
        if first:
            total[i] = summed
            acc[i] = picked
        else:
            total[i] = total[i] * shrink + summed
            acc[i] = acc[i] * shrink + picked

    def own_rows(i, carry):
        attend(normed_ref[i], col, i, True)
        return carry

    lax.fori_loop(0, rows, own_rows, 0, unroll=2)

    def arrived(step, carry):
        low, high = col - step, col + step
        for piece in range(PIECES):

            def rows_of(owner):
                def one(n, carry):
                    i = piece * part + n
                    attend(blocks[owner, i], owner, i, False)
                    return carry

                lax.fori_loop(0, part, one, 0, unroll=2)

            @pl.when(low >= 0)
            def _():
                piece_copy(low, piece, False, True).wait_recv()

                @pl.when(col < n_col - 1)
                def _():
                    piece_copy(low, piece, False, True).start()

            @pl.when(high < n_col)
            def _():
                piece_copy(high, piece, False, False).wait_recv()

                @pl.when(col > 0)
                def _():
                    piece_copy(high, piece, False, False).start()

            @pl.when(low >= 0)
            def _():
                rows_of(low)

            @pl.when(high < n_col)
            def _():
                rows_of(high)

        return carry

    lax.fori_loop(1, n_col, arrived, 0)

    def finish(i, carry):
        gate = jax.nn.sigmoid(
            jnp.dot(normed_ref[i], wg_ref[...], preferred_element_type=jnp.float32)
        )
        mean = acc[i] / total[i]
        stacked = jnp.concatenate(
            [
                jnp.concatenate(
                    [
                        mean[:, half * strip + h * rows : half * strip + (h + 1) * rows]
                        for half in range(halves)
                    ],
                    axis=1,
                )
                for h in range(n_heads)
            ],
            axis=0,
        )
        gated = (gate * stacked.T).astype(jnp.bfloat16)
        out_ref[i] = (
            pair_ref[i].astype(jnp.float32)
            + jnp.dot(gated, wo_ref[...], preferred_element_type=jnp.float32)
        ).astype(jnp.bfloat16)
        return carry

    lax.fori_loop(0, rows, finish, 0, unroll=2)

    @pl.when(col != home)
    def _():
        hop1(col).wait_send()

    @pl.when(col == home)
    def _():
        for step in range(1, groups):
            hop2(step).wait_send()

    hop3(core).wait_send()
    for piece in range(PIECES):
        for owner in range(n_col):

            @pl.when((owner <= col) & (col < n_col - 1))
            def _():
                piece_copy(owner, piece, False, True).wait_send()

            @pl.when((owner >= col) & (col > 0))
            def _():
                piece_copy(owner, piece, False, False).wait_send()


def attend(n_row, n_col, n_heads, normed, bias, pair, wq, wk, wvt, wg, wo):
    rows, cols, channels = normed.shape
    halves = cols // rows
    assert halves == 2 and cols % rows == 0 and n_row % 2 == 0
    groups = n_row // halves
    wide = cols * n_heads
    dma = pltpu.SemaphoreType.DMA
    vmem = pl.BlockSpec(memory_space=pltpu.VMEM)
    return pl.pallas_call(
        functools.partial(attend_kernel, n_row, n_col, n_heads),
        out_shape=jax.ShapeDtypeStruct(normed.shape, jnp.bfloat16),
        in_specs=[vmem] * 8,
        out_specs=vmem,
        scratch_shapes=[
            pltpu.VMEM((n_col,) + normed.shape, jnp.bfloat16),
            pltpu.VMEM((n_col,) + bias.shape, jnp.bfloat16),
            pltpu.VMEM((halves, n_col) + bias.shape, jnp.bfloat16),
            pltpu.VMEM((n_col, cols, wide), jnp.float32),
            pltpu.VMEM((rows, wide, channels), jnp.bfloat16),
            pltpu.VMEM((rows, 1, wide), jnp.float32),
            pltpu.VMEM((rows, 1, wide), jnp.float32),
            pltpu.VMEM((rows, channels // n_heads, wide), jnp.float32),
            dma,
            dma((n_col,)),
            dma((groups,)),
            dma,
            dma,
            dma,
            dma,
            dma((n_col, PIECES)),
            dma((n_col, PIECES)),
            dma((n_col, PIECES)),
        ],
        compiler_params=pltpu.CompilerParams(
            collective_id=1, has_side_effects=True, vmem_limit_bytes=48 * 2**20
        ),
        name="attend",
    )(normed, bias, pair, wq, wk, wvt, wg, wo)


def layer_norm(values, gain):
    center = values - jnp.mean(values, axis=-1, keepdims=True)
    spread = jnp.mean(center * center, axis=-1, keepdims=True)
    return center * lax.rsqrt(spread + 1e-05) * gain


def body(
    pair_in,
    coords,
    chain_ids,
    coord_mask,
    gain_tri,
    gain_sum,
    gain_attn,
    w_tri_in,
    w_tri_out,
    w_bins,
    same_chain,
    w_query,
    w_attn,
    w_bias,
    w_attn_out,
):
    row_count, col_count, channels = pair_in.shape
    n_heads = w_bias.shape[1]
    n_bins = w_bins.shape[0]
    col_start = lax.axis_index("col") * col_count
    coords_all, chains_all, masks_all = (
        lax.all_gather(coords, "row", axis=1, tiled=True),
        lax.all_gather(chain_ids, "row", axis=0, tiled=True),
        lax.all_gather(coord_mask, "row", axis=0, tiled=True),
    )
    pair_wide = pair_in.astype(jnp.float32)
    normed = layer_norm(pair_wide, gain_tri).astype(jnp.bfloat16)
    projected = jnp.dot(
        normed.reshape(row_count * col_count, channels),
        w_tri_in,
        preferred_element_type=jnp.float32,
    ).reshape(row_count, col_count, 5 * channels)
    left_side = (
        (jax.nn.sigmoid(projected[..., :channels]) * projected[..., channels : 2 * channels])
        .astype(jnp.bfloat16)
        .transpose(2, 0, 1)
    )
    right_side = (
        (
            jax.nn.sigmoid(projected[..., 2 * channels : 3 * channels])
            * projected[..., 3 * channels : 4 * channels]
        )
        .astype(jnp.bfloat16)
        .transpose(2, 0, 1)
    )
    tri_gate = jax.nn.sigmoid(projected[..., 4 * channels :])
    right_cols = lax.all_gather(right_side, "row", axis=1, tiled=True)
    summed = lax.psum_scatter(
        jnp.einsum(
            "cjk,cik->jci", right_cols, left_side, preferred_element_type=jnp.float32
        ).astype(jnp.bfloat16),
        "col",
        scatter_dimension=0,
        tiled=True,
    )
    product = summed.transpose(2, 0, 1).astype(jnp.float32)
    summed_norm = layer_norm(product, gain_sum).astype(jnp.bfloat16)
    pair_one = pair_wide + tri_gate * jnp.dot(
        summed_norm.reshape(row_count * col_count, channels),
        w_tri_out,
        preferred_element_type=jnp.float32,
    ).reshape(row_count, col_count, channels)
    far_coords = lax.dynamic_slice_in_dim(coords_all, col_start, col_count, 1)
    far_chains = lax.dynamic_slice_in_dim(chains_all, col_start, col_count, 0)
    far_masks = lax.dynamic_slice_in_dim(masks_all, col_start, col_count, 0)
    offsets = coords[:, :, None] - far_coords[:, None, :]
    dist = jnp.sqrt(jnp.sum(offsets * offsets, axis=0) + 1.0)
    centres = 2.0 + 20.0 * jnp.arange(n_bins, dtype=jnp.float32) / (n_bins - 1)
    spacing = 25.0 / (n_bins - 1)
    pair_mask = coord_mask.astype(jnp.float32)[:, None] * far_masks.astype(jnp.float32)[None, :]
    feats = jnp.exp(-(((dist[..., None] - centres) / spacing) ** 2)) * pair_mask[..., None]
    binned = jnp.dot(
        feats.reshape(row_count * col_count, n_bins), w_bins, precision=lax.Precision.HIGHEST
    ).reshape(row_count, col_count, channels)
    shared = (chain_ids[:, None] == far_chains[None, :]).astype(jnp.float32)
    pair_two = (pair_one + binned + shared[..., None] * same_chain).astype(jnp.bfloat16)
    normed_two = layer_norm(pair_two.astype(jnp.float32), gain_attn).astype(jnp.bfloat16)
    flat_two = normed_two.reshape(row_count * col_count, channels)
    pair_bias = (
        jnp.dot(flat_two, w_bias, preferred_element_type=jnp.float32)
        .astype(jnp.bfloat16)
        .reshape(row_count, col_count, n_heads)
        .transpose(1, 2, 0)
        .reshape(col_count, n_heads * row_count)
    )
    return attend(
        lax.axis_size("row"),
        lax.axis_size("col"),
        n_heads,
        normed_two,
        pair_bias,
        pair_two,
        w_query,
        w_attn[:, :channels],
        w_attn[:, channels : 2 * channels].T,
        w_attn[:, 2 * channels :],
        w_attn_out,
    )


def solution(mesh):
    return jax.shard_map(
        body,
        mesh=mesh,
        in_specs=(
            P("row", "col", None),
            P(None, "row"),
            P("row"),
            P("row"),
            P(),
            P(),
            P(),
            P(),
            P(),
            P(),
            P(),
            P(),
            P(),
            P(),
            P(),
        ),
        out_specs=P("row", "col", None),
        check_vma=False,
    )
```

time: 506 us -> 349 us (0.69)
  waiting for transfers between devices: 313 us -> 126 us
  Pallas kernels: 0 us -> 122 us
  matrix products: 69.3 us -> 22.6 us
  local copies, waits for them, and re-layouts: 46.4 us -> 30.6 us
  blocking collectives: 31.1 us -> 15.9 us
  other arithmetic: 29.3 us -> 16.8 us
    pallas_call x0 -> x1, Pallas kernels: none -> 122 us  [attend(): pl.pallas_call(functools.partial(attend_kernel, n_row, n_col, n_heads), o...]
    all_gather x2 -> x0, waiting for transfers between devices: 110 us -> none  [the longest x1 89.8 us: body(): panel = lax.all_gather(normed_two, 'col', axis=1, tiled=True)]
    reduce_scatter x1, waiting for transfers between devices: 142 us -> 66.5 us  [body(): lax.psum_scatter(jnp.einsum('cjk,cik->jci', right_cols, left_side, prefer...]
    dot_general x15 -> x0, matrix products: 45.7 us -> none  [the longest x6 18.7 us: one_block(): jnp.einsum('ihjk,ikhd->ihjd', expo.astype(jnp.bfloat16), value_blk, prefe...]
    all_gather x1 -> x0, blocking collectives: 15.3 us -> none  [body(): bias_wide = lax.all_gather(pair_bias, 'col', axis=2, tiled=True)]
    transpose x1 -> x0, local copies, waits for them, and re-layouts: 9.79 us -> none  [body(): jnp.einsum('cjk,cik->jci', right_cols, left_side, preferred_element_type=...]
    reduce_sum x6 -> x0, other arithmetic: 9.43 us -> none  [one_block(): new_total = running_total * rescale + jnp.sum(expo, axis=-1)]
    slice x1, local copies, waits for them, and re-layouts: 9.26 us -> 0.02 us  [body(): w_attn[:, 2 * channels:]]
  transfers between devices with their start and end apart: 4 -> 2, of which waited for: 4 -> 2; matrix products, arithmetic and copies ran while one was open for 2% -> 1% of each run, Pallas kernels for 0% -> 0%
where the time goes in v1:
time: 349 us; the launch traced here: 348 us
  waiting for transfers between devices  126 us (36%)
  Pallas kernels  122 us (35%)
  local copies, waits for them, and re-layouts  30.6 us (9%)
  matrix products  22.6 us (6%)
  other arithmetic  16.8 us (5%)
  blocking collectives  15.9 us (5%)
  between operations  14.4 us (4%)
    pallas_call x1, Pallas kernels, attend(): pl.pallas_call(functools.partial(attend_kernel, n_row, n_col, n_heads), o...  122 us
    reduce_scatter x1, waiting for transfers between devices, body(): lax.psum_scatter(jnp.einsum('cjk,cik->jci', right_cols, left_side, prefer...  66.5 us
    all_gather x1, waiting for transfers between devices, body(): right_cols = lax.all_gather(right_side, 'row', axis=1, tiled=True)  59.8 us
    all_gather x1, local copies, waits for them, and re-layouts, body(): right_cols = lax.all_gather(right_side, 'row', axis=1, tiled=True)  15.5 us
    dot_general x1, matrix products, body(): jnp.einsum('cjk,cik->jci', right_cols, left_side, preferred_element_type=...  12.7 us
    all_gather x1, blocking collectives, body(): lax.all_gather(coords, 'row', axis=1, tiled=True)  8.86 us
    convert_element_type x1, local copies, waits for them, and re-layouts, body(): summed = lax.psum_scatter(jnp.einsum('cjk,cik->jci', right_cols, left_sid...  7.51 us
    dot_general x1, matrix products, body(): jnp.dot(feats.reshape(row_count * col_count, n_bins), w_bins, precision=l...  7.05 us
  transfers between devices with their start and end apart: 2, of which 2 were waited for; matrix products, arithmetic and copies ran while one was open for 1% of the time, Pallas kernels for 0%

profile of v1, /device:TPU:0, one launch (start us, length us, event | category | flops | bytes accessed | tf_op | source)
XLA Modules:
  0.0 348.0 jit_solution(749655630732029143)
XLA Ops:
  6.5 1.9 convert_reduce_fusion
  8.4 2.7 fusion.4
  11.2 2.0 fusion.30
  13.2 2.7 fusion.38
  16.0 1.9 copy-done.3
  17.9 1.8 copy.58
  19.7 59.8 %all-gather.3.cloned.1.call-done = bf16[128,384,96]{0,2,1:T(8,128)(2,1)} async-done(((bf16[128,48,96]{0,2,1:T(8,128)(2,1)}), bf16[128,384,96]{0,2,1:T(8,128)(2,1)}) %all-gather.3.cloned.1.call-update) | async-done | bytes 9437200 | tf_op jit(solution)/shard_map/all_gather | solution.py:387
  79.5 15.5 %copy.59 = bf16[128,384,96]{2,1,0:T(8,128)(2,1)} copy(bf16[128,384,96]{0,2,1:T(8,128)(2,1)} %all-gather.3.cloned.1.call-done) | data formatting | bytes 18874368 | tf_op jit(solution)/shard_map/all_gather | solution.py:387
  94.9 12.7 %convert_bitcast_fusion = bf16[384,128,48]{0,2,1:T(8,128)(2,1)} fusion(bf16[128,48,96]{2,1,0:T(8,128)(2,1)} %copy.58, bf16[128,384,96]{2,1,0:T(8,128)(2,1)} %copy.59), kind=kOutput, calls=%fused_computation.1 | convolution fusion | flops 455344128 | bytes 15335424 | tf_op jit(solution)/shard_map/cjk,cik->jci/dot_general | solution.py:389
  107.6 7.5 %copy.60 = bf16[384,128,48]{1,2,0:T(8,128)(2,1)} copy(bf16[384,128,48]{0,2,1:T(8,128)(2,1)} %convert_bitcast_fusion) | data formatting | bytes 9437184 | tf_op jit(solution)/shard_map/convert_element_type | solution.py:391
  115.2 0.6 copy-done.8
  115.8 8.9 %all-gather = f32[8,48,3]{1,2,0:T(4,128)S(1)} all-gather(f32[1,48,3]{1,2,0:T(4,128)S(1)} %bitcast.52), channel_id=1, replica_groups=mesh['row'=8,'col'=4] {'row'}, dimensions={0}, use_global_device_ids=true | all-gather | bytes 5184 | tf_op jit(solution)/shard_map/all_gather | solution.py:362
  124.8 0.1 copy.69
  124.9 0.6 dynamic-slice
  126.2 0.2 dynamic-update-slice
  126.4 0.2 dynamic-update-slice.1
  126.6 7.0 %all-reduce.2 = (s32[384]{0:T(512)S(1)}, s32[384]{0:T(512)S(1)}) all-reduce(s32[384]{0:T(512)S(1)} %dynamic-update-slice.1, s32[384]{0:T(512)S(1)} %dynamic-update-slice), channel_id=1, replica_groups=mesh['row'=8,'col'=4] {'row'}, use_global_device_ids=true, to_apply=%add.1 | all-reduce | flops 768 | bytes 6144
  133.9 0.1 multiply_reduce_fusion
  134.1 66.5 %reduce-scatter.2.cloned.1.call-done = bf16[96,128,48]{1,2,0:T(8,128)(2,1)} async-done(((bf16[384,128,48]{1,2,0:T(8,128)(2,1)}), bf16[96,128,48]{1,2,0:T(8,128)(2,1)}) %reduce-scatter.2.cloned.1.call-update) | async-done | bytes 1179664 | tf_op jit(solution)/shard_map/reduce_scatter | solution.py:388
  200.6 2.0 bitcast_reduce_fusion
  202.8 2.5 fusion.27
  205.5 1.5 fusion.29
  207.0 0.5 fusion.32
  207.5 0.2 copy-done.14
  207.7 7.0 %convert_reduce_fusion.1 = (f32[48,96]{1,0:T(8,128)S(1)}, bf16[48,96,128]{2,1,0:T(8,128)(2,1)S(1)}) fusion(f32[128]{0:T(128)S(1)} %copy-done.16, f32[48,96]{1,0:T(8,128)S(1)} %compare_convert_fusion, f32[36,128]{1,0:T(8,128)S(1)} %copy-done.14, f32[48,96]{1,0:T(8,128)S(1)} %get-tuple-element.15, f32[36]{0:T(128)S(1)} %multiply_add_fusion, ...), kind=kOutput, calls=%fused_computation.6 | convolution fusion | flops 262706688 | bytes 7170704 | tf_op jit(solution)/shard_map/dot_general | solution.py:412
  214.8 1.6 fusion.7
  216.5 1.5 fusion.9.normed_ref
  218.0 0.4 convolution_convert_fusion
  218.4 0.1 reshape.146
  218.5 0.1 copy.68.bias_ref
  218.6 121.5 %attend.1 = bf16[48,96,128]{2,1,0:T(8,128)(2,1)S(1)} custom-call(bf16[48,96,128]{2,1,0:T(8,128)(2,1)S(1)} %fusion.9.normed_ref, bf16[96,192]{1,0:T(8,128)(2,1)S(1)} %copy.68.bias_ref, bf16[48,96,128]{2,1,0:T(8,128)(2,1)S(1)} %get-tuple-element.13.pair_ref, bf16[128,128]{1,0:T(8,128)(2,1)S(1)} %copy-done.1, bf16[128,128]{1,0:T(8,128)(2,1)S(1)} %get-tuple-element.10.wk_ref, ...), custom_call_target="tpu_custom_call" | custom-call | tf_op jit(solution)/shard_map/attend/pallas_call | solution.py:302
  340.2 1.0 copy.76
  (59 shorter events, 1.0 us)
Async XLA Ops:
  6.5 4.6 %copy-start = (bf16[128,640]{1,0:T(8,128)(2,1)S(1)}, bf16[128,640]{1,0:T(8,128)(2,1)}, u32[]{:S(2)}) copy-start(bf16[128,640]{1,0:T(8,128)(2,1)} %param.22) | copy-start | bytes 491524
  6.5 4.6 %copy-start.4 = (bf16[48,96,128]{2,1,0:T(8,128)(2,1)S(1)}, bf16[48,96,128]{2,1,0:T(8,128)(2,1)}, u32[]{:S(2)}) copy-start(bf16[48,96,128]{2,1,0:T(8,128)(2,1)} %param.15) | copy-start | bytes 3538948
  6.5 4.6 %copy-start.10 = (f32[128]{0:T(128)S(1)}, f32[128]{0:T(128)}, u32[]{:S(2)}) copy-start(f32[128]{0:T(128)} %param.19) | copy-start | bytes 1540
  6.5 72.9 %all-gather.3.cloned.1.call-start = ((), (), s32[]{:S(2)}) async-start(), calls=%async_computation.1 | async-start | bytes 10616832 | tf_op jit(solution)/shard_map/all_gather | solution.py:387
  13.2 4.6 %copy-start.3 = (f32[48,96,640]{2,1,0:T(8,128)}, f32[48,96,640]{2,1,0:T(8,128)S(1)}, u32[]{:S(2)}) copy-start(f32[48,96,640]{2,1,0:T(8,128)S(1)} %fusion.30) | copy-start | bytes 35389444
  17.9 182.7 %reduce-scatter.2.cloned.1.call-start = ((), (), s32[]{:S(2)}) async-start(), calls=%async_computation.2 | async-start | bytes 5898240 | tf_op jit(solution)/shard_map/reduce_scatter | solution.py:388
  115.1 0.7 copy-start.8
  115.1 9.6 %copy-start.15 = (s32[48]{0:T(128)S(1)}, s32[48]{0:T(128)}, u32[]{:S(2)}) copy-start(s32[48]{0:T(128)} %param.18) | copy-start | bytes 580
  115.1 9.6 %copy-start.6 = (bf16[128,384]{1,0:T(8,128)(2,1)S(1)}, bf16[128,384]{1,0:T(8,128)(2,1)}, u32[]{:S(2)}) copy-start(bf16[128,384]{1,0:T(8,128)(2,1)} %param.27) | copy-start | bytes 294916
  115.1 9.8 %copy-start.17 = (u32[32]{0:T(128)S(1)}, u32[32]{0:T(128)}, u32[]{:S(2)}) copy-start(u32[32]{0:T(128)} %constant.37) | copy-start | bytes 388
  115.1 11.3 %copy-start.11 = (s32[48]{0:T(128)S(1)}, s32[48]{0:T(128)}, u32[]{:S(2)}) copy-start(s32[48]{0:T(128)} %param.17) | copy-start | bytes 580
  115.1 90.4 %copy-start.12 = (f32[128]{0:T(128)S(1)}, f32[128]{0:T(128)}, u32[]{:S(2)}) copy-start(f32[128]{0:T(128)} %param.20) | copy-start | bytes 1540
  200.6 4.9 %copy-start.5 = (bf16[96,128,48]{1,2,0:T(8,128)(2,1)S(1)}, bf16[96,128,48]{1,2,0:T(8,128)(2,1)}, u32[]{:S(2)}) copy-start(bf16[96,128,48]{1,2,0:T(8,128)(2,1)} %reduce-scatter.2.cloned.1.call-done) | copy-start | bytes 3538948
  202.6 4.4 %copy-start.7 = (bf16[128,128]{1,0:T(8,128)(2,1)S(1)}, bf16[128,128]{1,0:T(8,128)(2,1)}, u32[]{:S(2)}) copy-start(bf16[128,128]{1,0:T(8,128)(2,1)} %param.23) | copy-start | bytes 98308
  207.0 0.7 copy-start.14
  207.0 0.7 copy-start.16
  207.7 8.8 %copy-start.13 = (f32[128]{0:T(128)S(1)}, f32[128]{0:T(128)}, u32[]{:S(2)}) copy-start(f32[128]{0:T(128)} %param.21) | copy-start | bytes 1540
  214.8 3.2 copy-start.9
  214.8 3.8 %copy-start.1 = (bf16[128,128]{1,0:T(8,128)(2,1)S(1)}, bf16[128,128]{1,0:T(8,128)(2,1)}, u32[]{:S(2)}) copy-start(bf16[128,128]{1,0:T(8,128)(2,1)} %wq_ref.1) | copy-start | bytes 98308
  214.8 3.8 %copy-start.2 = (bf16[128,128]{1,0:T(8,128)(2,1)S(1)}, bf16[128,128]{1,0:T(8,128)(2,1)}, u32[]{:S(2)}) copy-start(bf16[128,128]{1,0:T(8,128)(2,1)} %wo_ref.1) | copy-start | bytes 98308
Sparse Core Ops, SparseCore 0:
  18.0 61.4 all-gather.2
  115.3 85.2 reduce-scatter.1

commit v2 on v1

--- a/solution.py
+++ b/solution.py
@@ -15,6 +15,252 @@
 
 def contract_last(a, b):
     return lax.dot_general(a, b, (((1,), (1,)), ((), ())), preferred_element_type=jnp.float32)
+
+
+CHUNKS = 4
+
+
+def flip(index, bit):
+    return index + bit - 2 * bit * lax.rem(index // bit, 2)
+
+
+def routes(bits):
+    found = []
+    for offset in range(2, sum(bits) + 2, 2):
+        used = [n for n, bit in enumerate(bits) if offset & bit]
+        found.append((len(used), offset, bits[used[-1] + 1 :]))
+    return [(offset, later) for _, offset, later in sorted(found)]
+
+
+def triangle_kernel(
+    n_row,
+    n_col,
+    pack,
+    left_ref,
+    right_ref,
+    out_ref,
+    gathered,
+    left_wide,
+    sums,
+    land,
+    own_sem,
+    hop_send,
+    hop_recv,
+    up_send,
+    down_send,
+    sum_recv,
+):
+    row = lax.axis_index("row")
+    col = lax.axis_index("col")
+    groups, rows, depth = left_ref.shape
+    chunk = groups // CHUNKS
+    cols = depth // pack
+    halves = cols // rows
+    core = lax.rem(row, 2)
+    bits = [1 << n for n in range(1, n_row.bit_length() - 1)]
+    orders = (bits, bits[::-1])
+
+    barrier = pltpu.get_barrier_semaphore()
+    for step in range(1, n_row):
+        pl.semaphore_signal(
+            barrier, inc=1, device_id=(lax.rem(row + step, n_row), col), device_id_type=MESH
+        )
+    for step in range(1, n_col):
+        pl.semaphore_signal(
+            barrier, inc=1, device_id=(row, lax.rem(col + step, n_col)), device_id_type=MESH
+        )
+    pl.semaphore_wait(barrier, n_row - 1 + n_col - 1)
+
+    def hop(source, part, bit, own=False):
+        at = pl.ds(part * chunk, chunk)
+        return pltpu.make_async_remote_copy(
+            src_ref=right_ref.at[at] if own else gathered.at[source, at],
+            dst_ref=gathered.at[source, at],
+            send_sem=hop_send.at[bit.bit_length() - 1, source, part],
+            recv_sem=hop_recv.at[source, part],
+            device_id=(flip(row, bit), col),
+            device_id_type=MESH,
+        )
+
+    for part in range(CHUNKS):
+        for bit in bits + [1]:
+            hop(row, part, bit, True).start()
+    own_copy = pltpu.make_async_copy(right_ref, gathered.at[row], own_sem)
+    own_copy.start()
+
+    lane = lax.broadcasted_iota(jnp.int32, (rows, depth), 1) // cols
+
+    def widen(g, carry):
+        mine = left_ref[g].astype(jnp.float32)
+        for a in range(pack):
+            left_wide[g, a * rows : (a + 1) * rows, :] = jnp.where(lane == a, mine, 0.0).astype(
+                jnp.bfloat16
+            )
+        return carry
+
+    lax.fori_loop(0, groups, widen, 0)
+    own_copy.wait()
+
+    def source_of(offset):
+        source = row
+        for bit in bits + [1]:
+            if offset & bit:
+                source = flip(source, bit)
+        return source
+
+    def forward(part):
+        for parity in range(2):
+
+            @pl.when(core == parity)
+            def _():
+                for offset, later in routes(orders[parity]):
+                    source = source_of(offset)
+                    hop(source, part, 1).wait_recv()
+                    for bit in later + [1]:
+                        hop(source, part, bit).start()
+
+    def send_sum(dest, part, up):
+        at = pl.ds(part * chunk, chunk)
+        return pltpu.make_async_remote_copy(
+            src_ref=sums.at[dest, at],
+            dst_ref=land.at[dest + 1 if up else dest, at],
+            send_sem=(up_send if up else down_send).at[dest, part],
+            recv_sem=sum_recv.at[dest + 1 if up else dest, part],
+            device_id=(row, col + 1 if up else col - 1),
+            device_id_type=MESH,
+        )
+
+    def add_landed(dest, part, up):
+        send_sum(dest, part, up).wait_recv()
+        slot = dest + 1 if up else dest
+
+        def one(n, carry):
+            g = part * chunk + n
+            sums[dest, g] = (
+                sums[dest, g].astype(jnp.float32) + land[slot, g].astype(jnp.float32)
+            ).astype(jnp.bfloat16)
+            return carry
+
+        lax.fori_loop(0, chunk, one, 0)
+
+    forward(0)
+    for part in range(CHUNKS):
+        for offset in range(1, n_row, 2):
+            hop(source_of(offset), part, 1).wait_recv()
+
+        def partial(n, carry):
+            dest, g = n // chunk, part * chunk + lax.rem(n, chunk)
+            far = jnp.concatenate(
+                [gathered[dest * halves + half, g] for half in range(halves)], axis=0
+            )
+            sums[dest, g] = contract_last(far, left_wide[g]).astype(jnp.bfloat16)
+            return carry
+
+        lax.fori_loop(0, n_col * chunk, partial, 0)
+
+        @pl.when(col == 0)
+        def _():
+            for dest in range(n_col - 1, 0, -1):
+                send_sum(dest, part, True).start()
+
+        @pl.when(col == n_col - 1)
+        def _():
+            for dest in range(n_col - 1):
+                send_sum(dest, part, False).start()
+
+        if part + 1 < CHUNKS:
+            forward(part + 1)
+
+        for step in range(1, n_col):
+            high, low = n_col - step, step - 1
+
+            @pl.when((col < high) & (col > 0))
+            def _():
+                add_landed(high, part, True)
+                send_sum(high, part, True).start()
+
+            @pl.when((col > low) & (col < n_col - 1))
+            def _():
+                add_landed(low, part, False)
+                send_sum(low, part, False).start()
+
+        @pl.when(col > 0)
+        def _():
+            add_landed(col, part, True)
+
+        @pl.when(col < n_col - 1)
+        def _():
+            add_landed(col, part, False)
+
+    def store(g, carry):
+        out_ref[g] = sums[col, g]
+        return carry
+
+    lax.fori_loop(0, groups, store, 0)
+
+    for part in range(CHUNKS):
+        for bit in bits + [1]:
+            hop(row, part, bit, True).wait_send()
+        for parity in range(2):
+
+            @pl.when(core == parity)
+            def _():
+                for offset, later in routes(orders[parity]):
+                    for bit in later + [1]:
+                        hop(source_of(offset), part, bit).wait_send()
+
+        for dest in range(n_col):
+
+            @pl.when(col < dest)
+            def _():
+                send_sum(dest, part, True).wait_send()
+
+            @pl.when(col > dest)
+            def _():
+                send_sum(dest, part, False).wait_send()
+
+
+def triangle(n_row, n_col, left, right):
+    rows, cols, channels = left.shape
+    pack = 128 // math.gcd(rows, 128)
+    groups = channels // pack
+    assert cols == 2 * rows and groups % CHUNKS == 0 and n_row & (n_row - 1) == 0
+
+    def packed(side):
+        return (
+            side.reshape(rows, cols, pack, groups)
+            .transpose(3, 0, 2, 1)
+            .reshape(groups, rows, pack * cols)
+        )
+
+    dma = pltpu.SemaphoreType.DMA
+    vmem = pl.BlockSpec(memory_space=pltpu.VMEM)
+    block = (groups, cols, pack * rows)
+    summed = pl.pallas_call(
+        functools.partial(triangle_kernel, n_row, n_col, pack),
+        out_shape=jax.ShapeDtypeStruct(block, jnp.bfloat16),
+        in_specs=[vmem] * 2,
+        out_specs=vmem,
+        scratch_shapes=[
+            pltpu.VMEM((n_row, groups, rows, pack * cols), jnp.bfloat16),
+            pltpu.VMEM((groups, pack * rows, pack * cols), jnp.bfloat16),
+            pltpu.VMEM((n_col,) + block, jnp.bfloat16),
+            pltpu.VMEM((n_col + 1,) + block, jnp.bfloat16),
+            dma,
+            dma((n_row.bit_length() - 1, n_row, CHUNKS)),
+            dma((n_row, CHUNKS)),
+            dma((n_col, CHUNKS)),
+            dma((n_col, CHUNKS)),
+            dma((n_col + 1, CHUNKS)),
+        ],
+        compiler_params=pltpu.CompilerParams(
+            collective_id=2, has_side_effects=True, vmem_limit_bytes=58 * 2**20
+        ),
+        name="triangle",
+    )(packed(left), packed(right))
+    return (
+        summed.reshape(groups, cols, pack, rows).transpose(3, 1, 2, 0).reshape(rows, cols, channels)
+    )
 
 
 def attend_kernel(
@@ -371,29 +617,16 @@
         preferred_element_type=jnp.float32,
     ).reshape(row_count, col_count, 5 * channels)
     left_side = (
-        (jax.nn.sigmoid(projected[..., :channels]) * projected[..., channels : 2 * channels])
-        .astype(jnp.bfloat16)
-        .transpose(2, 0, 1)
+        jax.nn.sigmoid(projected[..., :channels]) * projected[..., channels : 2 * channels]
+    ).astype(jnp.bfloat16)
+    right_side = (
+        jax.nn.sigmoid(projected[..., 2 * channels : 3 * channels])
+        * projected[..., 3 * channels : 4 * channels]
+    ).astype(jnp.bfloat16)
+    tri_gate = jax.nn.sigmoid(projected[..., 4 * channels :])
+    product = triangle(lax.axis_size("row"), lax.axis_size("col"), left_side, right_side).astype(
+        jnp.float32
     )
-    right_side = (
-        (
-            jax.nn.sigmoid(projected[..., 2 * channels : 3 * channels])
-            * projected[..., 3 * channels : 4 * channels]
-        )
-        .astype(jnp.bfloat16)
-        .transpose(2, 0, 1)
-    )
-    tri_gate = jax.nn.sigmoid(projected[..., 4 * channels :])
-    right_cols = lax.all_gather(right_side, "row", axis=1, tiled=True)
-    summed = lax.psum_scatter(
-        jnp.einsum(
-            "cjk,cik->jci", right_cols, left_side, preferred_element_type=jnp.float32
-        ).astype(jnp.bfloat16),
-        "col",
-        scatter_dimension=0,
-        tiled=True,
-    )
-    product = summed.transpose(2, 0, 1).astype(jnp.float32)
     summed_norm = layer_norm(product, gain_sum).astype(jnp.bfloat16)
     pair_one = pair_wide + tri_gate * jnp.dot(
         summed_norm.reshape(row_count * col_count, channels),

time: 349 us -> 355 us (1.017)
  Pallas kernels: 122 us -> 298 us
  waiting for transfers between devices: 126 us -> 0 us
  local copies, waits for them, and re-layouts: 30.6 us -> 16.1 us
  between operations: 14.4 us -> 1.07 us
  matrix products: 22.6 us -> 11.8 us
  other arithmetic: 16.8 us -> 12.2 us
    pallas_call x0 -> x1, Pallas kernels: none -> 179 us  [triangle(): pl.pallas_call(functools.partial(triangle_kernel, n_row, n_col, pack), ou...]
    reduce_scatter x1 -> x0, waiting for transfers between devices: 66.5 us -> none  [body(): lax.psum_scatter(jnp.einsum('cjk,cik->jci', right_cols, left_side, prefer...]
    all_gather x1 -> x0, waiting for transfers between devices: 59.8 us -> none  [body(): right_cols = lax.all_gather(right_side, 'row', axis=1, tiled=True)]
    all_gather x1 -> x0, local copies, waits for them, and re-layouts: 15.5 us -> none  [body(): right_cols = lax.all_gather(right_side, 'row', axis=1, tiled=True)]
    dot_general x1 -> x0, matrix products: 12.7 us -> none  [body(): jnp.einsum('cjk,cik->jci', right_cols, left_side, preferred_element_type=...]
    reshape x0 -> x2, local copies, waits for them, and re-layouts: none -> 4.31 us  [packed(): return side.reshape(rows, cols, pack, groups).transpose(3, 0, 2, 1).resha...]
    convert_element_type x1 -> x4, local copies, waits for them, and re-layouts: 7.51 us -> 6.2 us  [the longest x2 3.48 us: body(): triangle(lax.axis_size('row'), lax.axis_size('col'), left_side, right_side)]
  transfers between devices with their start and end apart: 2 -> 0, of which waited for: 2 -> 0; matrix products, arithmetic and copies ran while one was open for 1% -> 0% of each run, Pallas kernels for 0% -> 0%
where the time goes in v2:
time: 355 us
  Pallas kernels  298 us (84%)
  local copies, waits for them, and re-layouts  16.1 us (5%)
  blocking collectives  15.3 us (4%)
  other arithmetic  12.2 us (3%)
  matrix products  11.8 us (3%)
    pallas_call x1, Pallas kernels, triangle(): pl.pallas_call(functools.partial(triangle_kernel, n_row, n_col, pack), ou...  179 us
    pallas_call x1, Pallas kernels, attend(): pl.pallas_call(functools.partial(attend_kernel, n_row, n_col, n_heads), o...  119 us
    all_gather x1, blocking collectives, body(): lax.all_gather(coords, 'row', axis=1, tiled=True)  9.68 us
    dot_general x1, matrix products, body(): jnp.dot(feats.reshape(row_count * col_count, n_bins), w_bins, precision=l...  7.29 us

profile of v2, /device:TPU:0, one launch (start us, length us, event | category | flops | bytes accessed | tf_op | source)
XLA Modules:
  0.0 354.9 jit_solution(3252011507591501105)
XLA Ops:
  0.0 1.9 convert_reduce_fusion
  1.9 2.7 fusion.7
  4.6 2.0 fusion.28
  6.7 2.7 fusion.16
  9.4 2.1 copy-done.3
  11.5 0.9 copy.42
  12.4 0.4 copy.43
  12.8 2.2 reshape.187.left_ref
  14.9 1.8 copy.44
  16.8 0.4 copy.45
  17.2 2.1 reshape.189.right_ref
  19.4 179.2 %triangle.1 = bf16[16,96,384]{2,1,0:T(8,128)(2,1)} custom-call(bf16[16,48,768]{2,1,0:T(8,128)(2,1)} %reshape.187.left_ref, bf16[16,48,768]{2,1,0:T(8,128)(2,1)} %reshape.189.right_ref), custom_call_target="tpu_custom_call" | custom-call | tf_op jit(solution)/shard_map/triangle/pallas_call | solution.py:239
  198.6 1.7 copy.46
  200.3 0.3 reduce_sum.65
  200.5 0.5 multiply_reduce_fusion
  201.0 1.8 copy.47
  202.9 0.7 fusion.2
  203.7 2.1 fusion.44
  205.8 0.6 dynamic-slice
  207.1 0.2 dynamic-update-slice
  207.3 0.2 dynamic-update-slice.1
  207.6 5.6 %all-reduce.2 = (s32[384]{0:T(512)S(1)}, s32[384]{0:T(512)S(1)}) all-reduce(s32[384]{0:T(512)S(1)} %dynamic-update-slice.1, s32[384]{0:T(512)S(1)} %dynamic-update-slice), channel_id=1, replica_groups=mesh['row'=8,'col'=4] {'row'}, use_global_device_ids=true, to_apply=%add.1 | all-reduce | flops 768 | bytes 6144
  213.2 9.7 %all-gather = f32[8,48,3]{1,2,0:T(4,128)S(1)} all-gather(f32[1,48,3]{1,2,0:T(4,128)S(1)} %bitcast.58), channel_id=1, replica_groups=mesh['row'=8,'col'=4] {'row'}, dimensions={0}, use_global_device_ids=true | all-gather | bytes 5184 | tf_op jit(solution)/shard_map/all_gather | solution.py:608
  223.5 7.3 %convert_reduce_fusion.1 = (f32[48,96]{1,0:T(8,128)S(1)}, bf16[48,96,128]{2,1,0:T(8,128)(2,1)S(1)}) fusion(f32[128]{0:T(128)S(1)} %copy-done.16, f32[48,96]{1,0:T(8,128)S(1)} %compare_convert_fusion, f32[36,128]{1,0:T(8,128)S(1)} %copy-done.14, f32[48,96]{1,0:T(8,128)S(1)} %get-tuple-element.15, f32[36]{0:T(128)S(1)} %multiply_add_fusion, ...), kind=kOutput, calls=%fused_computation.10 | convolution fusion | flops 262706688 | bytes 7170704 | tf_op jit(solution)/shard_map/dot_general | solution.py:645
  230.8 1.6 fusion.10
  232.5 1.5 fusion.12.normed_ref
  234.0 0.4 convolution_convert_fusion
  234.4 0.1 reshape.191
  234.5 0.1 copy.51.bias_ref
  234.6 0.1 copy.53
  234.8 119.1 %attend.1 = bf16[48,96,128]{2,1,0:T(8,128)(2,1)S(1)} custom-call(bf16[48,96,128]{2,1,0:T(8,128)(2,1)S(1)} %fusion.12.normed_ref, bf16[96,192]{1,0:T(8,128)(2,1)S(1)} %copy.51.bias_ref, bf16[48,96,128]{2,1,0:T(8,128)(2,1)S(1)} %get-tuple-element.13.pair_ref, bf16[128,128]{1,0:T(8,128)(2,1)S(1)} %copy-done.1, bf16[128,128]{1,0:T(8,128)(2,1)S(1)} %get-tuple-element.10.wk_ref, ...), custom_call_target="tpu_custom_call" | custom-call | tf_op jit(solution)/shard_map/attend/pallas_call | solution.py:548
  353.8 1.0 copy.58
  (54 shorter events, 0.8 us)
Async XLA Ops:
  0.0 4.6 %copy-start = (bf16[128,640]{1,0:T(8,128)(2,1)S(1)}, bf16[128,640]{1,0:T(8,128)(2,1)}, u32[]{:S(2)}) copy-start(bf16[128,640]{1,0:T(8,128)(2,1)} %param.22) | copy-start | bytes 491524
  0.0 4.6 %copy-start.4 = (bf16[48,96,128]{2,1,0:T(8,128)(2,1)S(1)}, bf16[48,96,128]{2,1,0:T(8,128)(2,1)}, u32[]{:S(2)}) copy-start(bf16[48,96,128]{2,1,0:T(8,128)(2,1)} %param.15) | copy-start | bytes 3538948
  0.0 4.6 %copy-start.10 = (f32[128]{0:T(128)S(1)}, f32[128]{0:T(128)}, u32[]{:S(2)}) copy-start(f32[128]{0:T(128)} %param.19) | copy-start | bytes 1540
  6.7 4.8 %copy-start.3 = (f32[48,96,640]{2,1,0:T(8,128)}, f32[48,96,640]{2,1,0:T(8,128)S(1)}, u32[]{:S(2)}) copy-start(f32[48,96,640]{2,1,0:T(8,128)S(1)} %fusion.28) | copy-start | bytes 35389444
  201.0 1.8 copy-start.11
  202.9 0.8 copy-start.7
  203.6 2.2 copy-start.17
  203.6 3.4 copy-start.15
  203.7 3.7 %copy-start.12 = (s32[48]{0:T(128)S(1)}, s32[48]{0:T(128)}, u32[]{:S(2)}) copy-start(s32[48]{0:T(128)} %param.17) | copy-start | bytes 580
  203.7 9.6 %copy-start.8 = (f32[3,48]{1,0:T(4,128)S(1)}, f32[3,48]{1,0:T(4,128)}, u32[]{:S(2)}) copy-start(f32[3,48]{1,0:T(4,128)} %param.16) | copy-start | bytes 1732
  203.7 19.7 %copy-start.5 = (bf16[48,96,128]{2,1,0:T(8,128)(2,1)S(1)}, bf16[48,96,128]{2,1,0:T(8,128)(2,1)}, u32[]{:S(2)}) copy-start(bf16[48,96,128]{2,1,0:T(8,128)(2,1)} %param.15) | copy-start | bytes 3538948
  203.7 19.7 %copy-start.14 = (f32[36,128]{1,0:T(8,128)S(1)}, f32[36,128]{1,0:T(8,128)}, u32[]{:S(2)}) copy-start(f32[36,128]{1,0:T(8,128)} %param.24) | copy-start | bytes 55300
  203.7 19.7 %copy-start.16 = (f32[128]{0:T(128)S(1)}, f32[128]{0:T(128)}, u32[]{:S(2)}) copy-start(f32[128]{0:T(128)} %param.25) | copy-start | bytes 1540
  223.4 9.0 %copy-start.13 = (f32[128]{0:T(128)S(1)}, f32[128]{0:T(128)}, u32[]{:S(2)}) copy-start(f32[128]{0:T(128)} %param.21) | copy-start | bytes 1540
  230.8 3.2 copy-start.9
  230.8 3.8 %copy-start.6 = (bf16[128,384]{1,0:T(8,128)(2,1)S(1)}, bf16[128,384]{1,0:T(8,128)(2,1)}, u32[]{:S(2)}) copy-start(bf16[128,384]{1,0:T(8,128)(2,1)} %param.27) | copy-start | bytes 294916
  232.4 2.3 copy-start.1
  232.5 2.3 copy-start.2

commit v3 on v2

--- a/solution.py
+++ b/solution.py
@@ -38,8 +38,13 @@
     pack,
     left_ref,
     right_ref,
+    facts_ref,
     out_ref,
+    facts_out,
     gathered,
+    facts,
+    facts_send,
+    facts_recv,
     left_wide,
     sums,
     land,
@@ -82,6 +87,18 @@
             device_id_type=MESH,
         )
 
+    def tell(target, source):
+        return pltpu.make_async_remote_copy(
+            src_ref=facts_ref,
+            dst_ref=facts.at[source],
+            send_sem=facts_send.at[target],
+            recv_sem=facts_recv.at[source],
+            device_id=(target, col),
+            device_id_type=MESH,
+        )
+
+    for step in range(1, n_row):
+        tell(lax.rem(row + step, n_row), row).start()
     for part in range(CHUNKS):
         for bit in bits + [1]:
             hop(row, part, bit, True).start()
@@ -143,20 +160,19 @@
 
         lax.fori_loop(0, chunk, one, 0)
 
-    forward(0)
-    for part in range(CHUNKS):
+    def multiply(part):
         for offset in range(1, n_row, 2):
             hop(source_of(offset), part, 1).wait_recv()
 
         def partial(n, carry):
-            dest, g = n // chunk, part * chunk + lax.rem(n, chunk)
-            far = jnp.concatenate(
-                [gathered[dest * halves + half, g] for half in range(halves)], axis=0
-            )
-            sums[dest, g] = contract_last(far, left_wide[g]).astype(jnp.bfloat16)
+            g = part * chunk + n
+            far = jnp.concatenate([gathered[source, g] for source in range(n_row)], axis=0)
+            found = contract_last(far, left_wide[g]).astype(jnp.bfloat16)
+            for dest in range(n_col):
+                sums[dest, g] = found[dest * cols : (dest + 1) * cols]
             return carry
 
-        lax.fori_loop(0, n_col * chunk, partial, 0)
+        lax.fori_loop(0, chunk, partial, 0)
 
         @pl.when(col == 0)
         def _():
@@ -171,6 +187,12 @@
         if part + 1 < CHUNKS:
             forward(part + 1)
 
+    forward(0)
+    multiply(0)
+    for part in range(CHUNKS):
+        if part + 1 < CHUNKS:
+            multiply(part + 1)
+
         for step in range(1, n_col):
             high, low = n_col - step, step - 1
 
@@ -197,6 +219,12 @@
         return carry
 
     lax.fori_loop(0, groups, store, 0)
+    facts_out[row] = facts_ref[...]
+    for step in range(1, n_row):
+        source = lax.rem(row + step, n_row)
+        tell(source, source).wait_recv()
+        facts_out[source] = facts[source]
+        tell(source, row).wait_send()
 
     for part in range(CHUNKS):
         for bit in bits + [1]:
@@ -220,7 +248,7 @@
                 send_sum(dest, part, False).wait_send()
 
 
-def triangle(n_row, n_col, left, right):
+def triangle(n_row, n_col, left, right, facts):
     rows, cols, channels = left.shape
     pack = 128 // math.gcd(rows, 128)
     groups = channels // pack
@@ -236,13 +264,19 @@
     dma = pltpu.SemaphoreType.DMA
     vmem = pl.BlockSpec(memory_space=pltpu.VMEM)
     block = (groups, cols, pack * rows)
-    summed = pl.pallas_call(
+    summed, facts_all = pl.pallas_call(
         functools.partial(triangle_kernel, n_row, n_col, pack),
-        out_shape=jax.ShapeDtypeStruct(block, jnp.bfloat16),
-        in_specs=[vmem] * 2,
-        out_specs=vmem,
+        out_shape=[
+            jax.ShapeDtypeStruct(block, jnp.bfloat16),
+            jax.ShapeDtypeStruct((n_row,) + facts.shape, jnp.float32),
+        ],
+        in_specs=[vmem] * 3,
+        out_specs=[vmem] * 2,
         scratch_shapes=[
             pltpu.VMEM((n_row, groups, rows, pack * cols), jnp.bfloat16),
+            pltpu.VMEM((n_row,) + facts.shape, jnp.float32),
+            dma((n_row,)),
+            dma((n_row,)),
             pltpu.VMEM((groups, pack * rows, pack * cols), jnp.bfloat16),
             pltpu.VMEM((n_col,) + block, jnp.bfloat16),
             pltpu.VMEM((n_col + 1,) + block, jnp.bfloat16),
@@ -257,10 +291,11 @@
             collective_id=2, has_side_effects=True, vmem_limit_bytes=58 * 2**20
         ),
         name="triangle",
-    )(packed(left), packed(right))
-    return (
+    )(packed(left), packed(right), facts)
+    product = (
         summed.reshape(groups, cols, pack, rows).transpose(3, 1, 2, 0).reshape(rows, cols, channels)
     )
+    return product, facts_all[:, :, :rows].transpose(1, 0, 2).reshape(facts.shape[0], -1)
 
 
 def attend_kernel(
@@ -604,11 +639,15 @@
     n_heads = w_bias.shape[1]
     n_bins = w_bins.shape[0]
     col_start = lax.axis_index("col") * col_count
-    coords_all, chains_all, masks_all = (
-        lax.all_gather(coords, "row", axis=1, tiled=True),
-        lax.all_gather(chain_ids, "row", axis=0, tiled=True),
-        lax.all_gather(coord_mask, "row", axis=0, tiled=True),
+    facts = jnp.concatenate(
+        [
+            coords,
+            chain_ids.astype(jnp.float32)[None],
+            coord_mask.astype(jnp.float32)[None],
+        ],
+        axis=0,
     )
+    facts = jnp.pad(facts, ((0, -facts.shape[0] % 8), (0, -row_count % 128)))
     pair_wide = pair_in.astype(jnp.float32)
     normed = layer_norm(pair_wide, gain_tri).astype(jnp.bfloat16)
     projected = jnp.dot(
@@ -624,28 +663,28 @@
         * projected[..., 3 * channels : 4 * channels]
     ).astype(jnp.bfloat16)
     tri_gate = jax.nn.sigmoid(projected[..., 4 * channels :])
-    product = triangle(lax.axis_size("row"), lax.axis_size("col"), left_side, right_side).astype(
-        jnp.float32
+    product, facts_all = triangle(
+        lax.axis_size("row"), lax.axis_size("col"), left_side, right_side, facts
     )
+    product = product.astype(jnp.float32)
     summed_norm = layer_norm(product, gain_sum).astype(jnp.bfloat16)
     pair_one = pair_wide + tri_gate * jnp.dot(
         summed_norm.reshape(row_count * col_count, channels),
         w_tri_out,
         preferred_element_type=jnp.float32,
     ).reshape(row_count, col_count, channels)
-    far_coords = lax.dynamic_slice_in_dim(coords_all, col_start, col_count, 1)
-    far_chains = lax.dynamic_slice_in_dim(chains_all, col_start, col_count, 0)
-    far_masks = lax.dynamic_slice_in_dim(masks_all, col_start, col_count, 0)
+    far_facts = lax.dynamic_slice_in_dim(facts_all, col_start, col_count, 1)
+    far_coords, far_chains, far_masks = far_facts[:3], far_facts[3], far_facts[4]
     offsets = coords[:, :, None] - far_coords[:, None, :]
     dist = jnp.sqrt(jnp.sum(offsets * offsets, axis=0) + 1.0)
     centres = 2.0 + 20.0 * jnp.arange(n_bins, dtype=jnp.float32) / (n_bins - 1)
     spacing = 25.0 / (n_bins - 1)
-    pair_mask = coord_mask.astype(jnp.float32)[:, None] * far_masks.astype(jnp.float32)[None, :]
+    pair_mask = coord_mask.astype(jnp.float32)[:, None] * far_masks[None, :]
     feats = jnp.exp(-(((dist[..., None] - centres) / spacing) ** 2)) * pair_mask[..., None]
     binned = jnp.dot(
         feats.reshape(row_count * col_count, n_bins), w_bins, precision=lax.Precision.HIGHEST
     ).reshape(row_count, col_count, channels)
-    shared = (chain_ids[:, None] == far_chains[None, :]).astype(jnp.float32)
+    shared = (chain_ids.astype(jnp.float32)[:, None] == far_chains[None, :]).astype(jnp.float32)
     pair_two = (pair_one + binned + shared[..., None] * same_chain).astype(jnp.bfloat16)
     normed_two = layer_norm(pair_two.astype(jnp.float32), gain_attn).astype(jnp.bfloat16)
     flat_two = normed_two.reshape(row_count * col_count, channels)

time: 355 us -> 314 us (0.88)
  Pallas kernels: 298 us -> 272 us
  blocking collectives: 15.3 us -> 0 us
    pallas_call x1, Pallas kernels: 179 us -> 155 us  [triangle(): pl.pallas_call(functools.partial(triangle_kernel, n_row, n_col, pack), ou...]
    all_gather x1 -> x0, blocking collectives: 9.68 us -> none  [body(): lax.all_gather(coords, 'row', axis=1, tiled=True)]
    unnamed x1 -> x0, blocking collectives: 5.59 us -> none
where the time goes in v3:
time: 314 us
  Pallas kernels  272 us (87%)
  local copies, waits for them, and re-layouts  15 us (5%)
  other arithmetic  14.1 us (4%)
  matrix products  11.8 us (4%)
    pallas_call x1, Pallas kernels, triangle(): pl.pallas_call(functools.partial(triangle_kernel, n_row, n_col, pack), ou...  155 us
    pallas_call x1, Pallas kernels, attend(): pl.pallas_call(functools.partial(attend_kernel, n_row, n_col, n_heads), o...  118 us
    dot_general x1, matrix products, body(): jnp.dot(feats.reshape(row_count * col_count, n_bins), w_bins, precision=l...  7.29 us

profile of v3, /device:TPU:0, one launch (start us, length us, event | category | flops | bytes accessed | tf_op | source)
XLA Modules:
  0.0 313.9 jit_solution(1148877506008674281)
XLA Ops:
  0.0 0.8 fusion.49
  0.8 1.3 select_maximum_fusion.facts_ref
  2.1 1.8 convert_reduce_fusion
  3.8 2.7 fusion.7
  6.6 2.0 fusion.28
  8.7 2.7 fusion.16
  11.4 2.1 copy-done.3
  13.4 0.9 copy.32
  14.3 0.4 copy.33
  14.7 2.2 reshape.194.left_ref
  16.9 1.8 copy.34
  18.8 0.4 copy.35
  19.2 2.1 reshape.196.right_ref
  21.3 154.9 %triangle.1 = (bf16[16,96,384]{2,1,0:T(8,128)(2,1)}, f32[8,8,128]{2,1,0:T(8,128)}) custom-call(bf16[16,48,768]{2,1,0:T(8,128)(2,1)} %reshape.194.left_ref, bf16[16,48,768]{2,1,0:T(8,128)(2,1)} %reshape.196.right_ref, f32[8,128]{1,0:T(8,128)} %select_maximum_fusion.facts_ref), custom_call_target="tpu_custom_call" | custom-call | tf_op jit(solution)/shard_map/triangle/pallas_call | solution.py:267
  176.2 1.7 copy.36
  177.8 0.3 reduce_sum.65
  178.1 0.5 multiply_reduce_fusion
  178.6 1.8 copy.37
  180.5 0.7 fusion.2
  181.3 2.1 fusion.44
  183.4 0.1 reshape.197
  183.6 0.1 broadcast_multiply_fusion
  183.7 0.1 multiply_reduce_fusion.1
  183.9 7.3 %convert_reduce_fusion.1 = (f32[48,96]{1,0:T(8,128)S(1)}, bf16[48,96,128]{2,1,0:T(8,128)(2,1)S(1)}) fusion(f32[128]{0:T(128)S(1)} %copy-done.15, f32[48,96]{1,0:T(8,128)S(1)} %compare_convert_fusion, f32[36,128]{1,0:T(8,128)S(1)} %copy-done.14, f32[48,96]{1,0:T(8,128)S(1)} %broadcast_multiply_fusion, f32[36]{0:T(128)S(1)} %multiply_add_fusion, ...), kind=kOutput, calls=%fused_computation.10 | convolution fusion | flops 262706688 | bytes 7170704 | tf_op jit(solution)/shard_map/dot_general | solution.py:684
  191.2 1.6 fusion.10
  192.9 1.5 fusion.12.normed_ref
  194.4 0.4 convolution_convert_fusion
  194.8 0.1 reshape.199
  194.9 0.1 copy.41.bias_ref
  195.1 0.1 copy.43
  195.2 117.6 %attend.1 = bf16[48,96,128]{2,1,0:T(8,128)(2,1)S(1)} custom-call(bf16[48,96,128]{2,1,0:T(8,128)(2,1)S(1)} %fusion.12.normed_ref, bf16[96,192]{1,0:T(8,128)(2,1)S(1)} %copy.41.bias_ref, bf16[48,96,128]{2,1,0:T(8,128)(2,1)S(1)} %get-tuple-element.21.pair_ref, bf16[128,128]{1,0:T(8,128)(2,1)S(1)} %copy-done.1, bf16[128,128]{1,0:T(8,128)(2,1)S(1)} %get-tuple-element.12.wk_ref, ...), custom_call_target="tpu_custom_call" | custom-call | tf_op jit(solution)/shard_map/attend/pallas_call | solution.py:583
  312.8 1.0 copy.45
  (46 shorter events, 0.4 us)
Async XLA Ops:
  0.0 6.6 %copy-start = (bf16[128,640]{1,0:T(8,128)(2,1)S(1)}, bf16[128,640]{1,0:T(8,128)(2,1)}, u32[]{:S(2)}) copy-start(bf16[128,640]{1,0:T(8,128)(2,1)} %param.22) | copy-start | bytes 491524
  0.0 6.6 %copy-start.4 = (bf16[48,96,128]{2,1,0:T(8,128)(2,1)S(1)}, bf16[48,96,128]{2,1,0:T(8,128)(2,1)}, u32[]{:S(2)}) copy-start(bf16[48,96,128]{2,1,0:T(8,128)(2,1)} %param.15) | copy-start | bytes 3538948
  0.0 6.6 %copy-start.11 = (f32[128]{0:T(128)S(1)}, f32[128]{0:T(128)}, u32[]{:S(2)}) copy-start(f32[128]{0:T(128)} %param.19) | copy-start | bytes 1540
  8.6 4.8 %copy-start.3 = (f32[48,96,640]{2,1,0:T(8,128)}, f32[48,96,640]{2,1,0:T(8,128)S(1)}, u32[]{:S(2)}) copy-start(f32[48,96,640]{2,1,0:T(8,128)S(1)} %fusion.28) | copy-start | bytes 35389444
  178.6 1.8 copy-start.12
  180.5 0.8 copy-start.7
  181.2 2.2 copy-start.8
  181.2 2.5 copy-start.9
  181.2 2.6 copy-start.5
  181.2 2.6 copy-start.14
  181.3 2.6 copy-start.15
  183.9 9.0 %copy-start.13 = (f32[128]{0:T(128)S(1)}, f32[128]{0:T(128)}, u32[]{:S(2)}) copy-start(f32[128]{0:T(128)} %param.21) | copy-start | bytes 1540
  191.2 3.2 %copy-start.10 = (bf16[128,4]{0,1:T(4,128)(2,1)S(1)}, bf16[128,4]{0,1:T(4,128)(2,1)}, u32[]{:S(2)}) copy-start(bf16[128,4]{0,1:T(4,128)(2,1)} %param.28) | copy-start | bytes 3076
  191.2 3.8 %copy-start.6 = (bf16[128,384]{1,0:T(8,128)(2,1)S(1)}, bf16[128,384]{1,0:T(8,128)(2,1)}, u32[]{:S(2)}) copy-start(bf16[128,384]{1,0:T(8,128)(2,1)} %param.27) | copy-start | bytes 294916
  192.9 2.3 copy-start.1
  192.9 2.3 copy-start.2

commit v4 on v3

--- a/solution.py
+++ b/solution.py
@@ -99,7 +99,7 @@
 
     for step in range(1, n_row):
         tell(lax.rem(row + step, n_row), row).start()
-    for part in range(CHUNKS):
+    for part in range(min(2, CHUNKS)):
         for bit in bits + [1]:
             hop(row, part, bit, True).start()
     own_copy = pltpu.make_async_copy(right_ref, gathered.at[row], own_sem)
@@ -135,6 +135,10 @@
                     hop(source, part, 1).wait_recv()
                     for bit in later + [1]:
                         hop(source, part, bit).start()
+
+        if part + 2 < CHUNKS:
+            for bit in bits + [1]:
+                hop(row, part + 2, bit, True).start()
 
     def send_sum(dest, part, up):
         at = pl.ds(part * chunk, chunk)
@@ -481,6 +485,28 @@
         attend(normed_ref[i], col, i, True)
         return carry
 
+    def pass_on(step, piece):
+        low, high = col - step, col + step
+
+        @pl.when(low >= 0)
+        def _():
+            piece_copy(low, piece, False, True).wait_recv()
+
+            @pl.when(col < n_col - 1)
+            def _():
+                piece_copy(low, piece, False, True).start()
+
+        @pl.when(high < n_col)
+        def _():
+            piece_copy(high, piece, False, False).wait_recv()
+
+            @pl.when(col > 0)
+            def _():
+                piece_copy(high, piece, False, False).start()
+
+    for piece in range(PIECES):
+        pass_on(1, piece)
+
     lax.fori_loop(0, rows, own_rows, 0, unroll=2)
 
     def arrived(step, carry):
@@ -495,21 +521,9 @@
 
                 lax.fori_loop(0, part, one, 0, unroll=2)
 
-            @pl.when(low >= 0)
-            def _():
-                piece_copy(low, piece, False, True).wait_recv()
-
-                @pl.when(col < n_col - 1)
-                def _():
-                    piece_copy(low, piece, False, True).start()
-
-            @pl.when(high < n_col)
-            def _():
-                piece_copy(high, piece, False, False).wait_recv()
-
-                @pl.when(col > 0)
-                def _():
-                    piece_copy(high, piece, False, False).start()
+            @pl.when(step > 1)
+            def _():
+                pass_on(step, piece)
 
             @pl.when(low >= 0)
             def _():

time: 314 us -> 321 us (1.022)
  Pallas kernels: 272 us -> 279 us
    pallas_call x1, Pallas kernels: 118 us -> 136 us  [attend(): pl.pallas_call(functools.partial(attend_kernel, n_row, n_col, n_heads), o...]
    pallas_call x1, Pallas kernels: 155 us -> 143 us  [triangle(): pl.pallas_call(functools.partial(triangle_kernel, n_row, n_col, pack), ou...]
where the time goes in v4:
time: 321 us
  Pallas kernels  279 us (87%)
  local copies, waits for them, and re-layouts  15 us (5%)
  other arithmetic  14.1 us (4%)
  matrix products  11.8 us (4%)
    pallas_call x1, Pallas kernels, triangle(): pl.pallas_call(functools.partial(triangle_kernel, n_row, n_col, pack), ou...  143 us
    pallas_call x1, Pallas kernels, attend(): pl.pallas_call(functools.partial(attend_kernel, n_row, n_col, n_heads), o...  136 us
    dot_general x1, matrix products, body(): jnp.dot(feats.reshape(row_count * col_count, n_bins), w_bins, precision=l...  7.29 us

profile of v4, /device:TPU:0, one launch (start us, length us, event | category | flops | bytes accessed | tf_op | source)
XLA Modules:
  0.0 320.6 jit_solution(6559255479733440023)
XLA Ops:
  0.0 0.8 fusion.49
  0.8 1.3 select_maximum_fusion.facts_ref
  2.1 1.8 convert_reduce_fusion
  3.8 2.7 fusion.7
  6.6 2.0 fusion.28
  8.7 2.7 fusion.16
  11.4 2.1 copy-done.3
  13.4 0.9 copy.32
  14.3 0.4 copy.33
  14.7 2.2 reshape.194.left_ref
  16.9 1.8 copy.34
  18.8 0.4 copy.35
  19.2 2.1 reshape.196.right_ref
  21.3 142.8 %triangle.1 = (bf16[16,96,384]{2,1,0:T(8,128)(2,1)}, f32[8,8,128]{2,1,0:T(8,128)}) custom-call(bf16[16,48,768]{2,1,0:T(8,128)(2,1)} %reshape.194.left_ref, bf16[16,48,768]{2,1,0:T(8,128)(2,1)} %reshape.196.right_ref, f32[8,128]{1,0:T(8,128)} %select_maximum_fusion.facts_ref), custom_call_target="tpu_custom_call" | custom-call | tf_op jit(solution)/shard_map/triangle/pallas_call | solution.py:271
  164.1 1.7 copy.36
  165.8 0.3 reduce_sum.65
  166.1 0.5 multiply_reduce_fusion
  166.6 1.8 copy.37
  168.4 0.7 fusion.2
  169.2 2.1 fusion.44
  171.4 0.1 reshape.197
  171.5 0.1 broadcast_multiply_fusion
  171.7 0.1 multiply_reduce_fusion.1
  171.9 7.3 %convert_reduce_fusion.1 = (f32[48,96]{1,0:T(8,128)S(1)}, bf16[48,96,128]{2,1,0:T(8,128)(2,1)S(1)}) fusion(f32[128]{0:T(128)S(1)} %copy-done.15, f32[48,96]{1,0:T(8,128)S(1)} %compare_convert_fusion, f32[36,128]{1,0:T(8,128)S(1)} %copy-done.14, f32[48,96]{1,0:T(8,128)S(1)} %broadcast_multiply_fusion, f32[36]{0:T(128)S(1)} %multiply_add_fusion, ...), kind=kOutput, calls=%fused_computation.10 | convolution fusion | flops 262706688 | bytes 7170704 | tf_op jit(solution)/shard_map/dot_general | solution.py:698
  179.2 1.6 fusion.10
  180.9 1.5 fusion.12.normed_ref
  182.4 0.4 convolution_convert_fusion
  182.8 0.1 reshape.199
  182.9 0.1 copy.41.bias_ref
  183.0 0.1 copy.43
  183.2 136.4 %attend.1 = bf16[48,96,128]{2,1,0:T(8,128)(2,1)S(1)} custom-call(bf16[48,96,128]{2,1,0:T(8,128)(2,1)S(1)} %fusion.12.normed_ref, bf16[96,192]{1,0:T(8,128)(2,1)S(1)} %copy.41.bias_ref, bf16[48,96,128]{2,1,0:T(8,128)(2,1)S(1)} %get-tuple-element.21.pair_ref, bf16[128,128]{1,0:T(8,128)(2,1)S(1)} %copy-done.1, bf16[128,128]{1,0:T(8,128)(2,1)S(1)} %get-tuple-element.12.wk_ref, ...), custom_call_target="tpu_custom_call" | custom-call | tf_op jit(solution)/shard_map/attend/pallas_call | solution.py:597
  319.6 1.0 copy.45
  (46 shorter events, 0.4 us)
Async XLA Ops:
  0.0 6.6 %copy-start = (bf16[128,640]{1,0:T(8,128)(2,1)S(1)}, bf16[128,640]{1,0:T(8,128)(2,1)}, u32[]{:S(2)}) copy-start(bf16[128,640]{1,0:T(8,128)(2,1)} %param.22) | copy-start | bytes 491524
  0.0 6.6 %copy-start.4 = (bf16[48,96,128]{2,1,0:T(8,128)(2,1)S(1)}, bf16[48,96,128]{2,1,0:T(8,128)(2,1)}, u32[]{:S(2)}) copy-start(bf16[48,96,128]{2,1,0:T(8,128)(2,1)} %param.15) | copy-start | bytes 3538948
  0.0 6.6 %copy-start.11 = (f32[128]{0:T(128)S(1)}, f32[128]{0:T(128)}, u32[]{:S(2)}) copy-start(f32[128]{0:T(128)} %param.19) | copy-start | bytes 1540
  8.6 4.8 %copy-start.3 = (f32[48,96,640]{2,1,0:T(8,128)}, f32[48,96,640]{2,1,0:T(8,128)S(1)}, u32[]{:S(2)}) copy-start(f32[48,96,640]{2,1,0:T(8,128)S(1)} %fusion.28) | copy-start | bytes 35389444
  166.6 1.8 copy-start.12
  168.4 0.8 copy-start.7
  169.2 2.2 copy-start.8
  169.2 2.5 copy-start.9
  169.2 2.6 copy-start.5
  169.2 2.6 copy-start.14
  169.2 2.6 copy-start.15
  171.8 9.0 %copy-start.13 = (f32[128]{0:T(128)S(1)}, f32[128]{0:T(128)}, u32[]{:S(2)}) copy-start(f32[128]{0:T(128)} %param.21) | copy-start | bytes 1540
  179.2 3.2 copy-start.10
  179.2 3.8 %copy-start.6 = (bf16[128,384]{1,0:T(8,128)(2,1)S(1)}, bf16[128,384]{1,0:T(8,128)(2,1)}, u32[]{:S(2)}) copy-start(bf16[128,384]{1,0:T(8,128)(2,1)} %param.27) | copy-start | bytes 294916
  180.8 2.3 copy-start.1
  180.8 2.3 copy-start.2
